TPU v7x, 32 devices: a whole 2x2x4 slice. The times are simulated.
32 devices in a mesh: pipe: 4 (over y, x), dp: 8 (over z, core).
Axes of the slice: x: 2, y: 2, z: 4, core: 2. Of those that a mesh axis runs over, the one named last changes fastest.
Arguments:
- inputs: bfloat16 [6, 256, 8192], P(None, 'dp'), may hold values from -6 to 6
- cotangent: bfloat16 [6, 256, 8192], P(None, 'dp'), may hold values from -0.19921875 to 0.19921875
- plan_order: int32 [6], replicated, may hold values from 0 to 5, each once
- norm_gain: float32 [4, 8192], P('pipe'), may hold values from 0.5 to 1.5
- weight_in: bfloat16 [4, 8192, 512], P('pipe'), may hold values from -0.0625 to 0.0625
- weight_out: bfloat16 [4, 512, 8192], P('pipe'), may hold values from -0.25 to 0.25
Outputs:
- grad_in: bfloat16 [4, 8192, 512], P('pipe', 'dp')
- grad_out: bfloat16 [4, 512, 8192], P('pipe', None, 'dp')
Inputs may be any that keep to these rules, and one draw needn't show every extreme that they name: plan_order names each slot's sample once: a permutation.
All inputs are finite; a program needn't handle non-finite values.
Results may differ from a plain program's by a relative error of at most 0.024.
Values may be sent and summed in bfloat16 or wider, within the bound.
A program may use at most 128 MiB of HBM per device.

v0:
```python
import jax
import jax.numpy as jnp
from jax import lax
from jax.sharding import PartitionSpec as P

EPSILON = 1e-05


def passed_along(value, axis, by):
    length = lax.axis_size(axis)
    pairs = [(i, i + by) for i in range(length) if 0 <= i + by < length]
    return lax.ppermute(value, axis, pairs)


def inner_section(rows_in, gain_row, weight_first):
    float_cast = rows_in.astype(jnp.float32)
    inverse_root_mean = lax.rsqrt(
        jnp.mean(float_cast * float_cast, axis=-1, keepdims=True) + EPSILON
    )
    normed = (float_cast * inverse_root_mean * gain_row).astype(jnp.bfloat16)
    pre_act = jnp.dot(normed, weight_first, preferred_element_type=jnp.float32)
    hidden = jax.nn.silu(pre_act).astype(jnp.bfloat16)
    return (float_cast, inverse_root_mean, normed, pre_act, hidden)


def backward_section(
    float_cast, inverse_root_mean, pre_act, incoming_gradient, gain_row, weight_first, weight_second
):
    grad_hidden = jnp.einsum(
        "td,rd->tr", incoming_gradient, weight_second, preferred_element_type=jnp.float32
    )
    sigmoid_pre = jax.nn.sigmoid(pre_act)
    grad_pre = (grad_hidden * sigmoid_pre * (1.0 + pre_act * (1.0 - sigmoid_pre))).astype(
        jnp.bfloat16
    )
    back_rows = jnp.einsum("tr,dr->td", grad_pre, weight_first, preferred_element_type=jnp.float32)
    normalized_input = float_cast * inverse_root_mean
    rescaled_rows = back_rows * gain_row
    grad_rows = incoming_gradient.astype(jnp.float32) + inverse_root_mean * (
        rescaled_rows
        - normalized_input * jnp.mean(rescaled_rows * normalized_input, axis=-1, keepdims=True)
    )
    return (grad_rows.astype(jnp.bfloat16), grad_pre)


def pick_slot(buffer, slot_index):
    return lax.dynamic_index_in_dim(buffer, slot_index, 0, keepdims=False)


def put_slot(buffer, new_value, slot_index, active_flag):
    previous = pick_slot(buffer, slot_index)
    return lax.dynamic_update_index_in_dim(
        buffer, jnp.where(active_flag, new_value, previous), slot_index, 0
    )


def per_device(inputs, cotangent, plan_order, norm_gain, weight_in, weight_out):
    gain_row = norm_gain[0]
    weight_first = weight_in[0]
    weight_second = weight_out[0]
    sections = lax.axis_size("pipe")
    section_index = lax.axis_index("pipe")
    micro_count, row_count, model_width = inputs.shape
    inner_width = weight_first.shape[1]
    tick_count = micro_count + sections - 1

    def buffer(columns, dtype):
        return jnp.zeros((micro_count, row_count, columns), dtype)

    extras = ()

    def forward_tick(moment, state_tuple):
        outgoing, kept_rows, kept_extra = state_tuple
        arrived = passed_along(outgoing, "pipe", 1)
        position = moment - section_index
        active_flag = (position >= 0) & (position < micro_count)
        slot_index = jnp.clip(position, 0, micro_count - 1)
        fresh_rows = pick_slot(inputs, plan_order[slot_index])
        rows_in = jnp.where(section_index == 0, fresh_rows, arrived)
        float_cast, inverse_root_mean, normed, pre_act, hidden = inner_section(
            rows_in, gain_row, weight_first
        )
        result = (
            float_cast + jnp.dot(hidden, weight_second, preferred_element_type=jnp.float32)
        ).astype(jnp.bfloat16)
        kept_rows = put_slot(kept_rows, rows_in, slot_index, active_flag)
        return (result, kept_rows, kept_extra)

    empty_rows = jnp.zeros((row_count, model_width), jnp.bfloat16)
    unused, kept_rows, extras = lax.fori_loop(
        0, tick_count, forward_tick, (empty_rows, buffer(model_width, jnp.bfloat16), extras)
    )
    normed_start = buffer(model_width, jnp.bfloat16)
    hidden_start = buffer(inner_width, jnp.bfloat16)

    def backward_tick(moment, state_tuple):
        outgoing, normed_all, hidden_gathered, grad_all, upstream_all = state_tuple
        arrived = passed_along(outgoing, "pipe", -1)
        position = moment - (sections - 1 - section_index)
        active_flag = (position >= 0) & (position < micro_count)
        slot_index = jnp.clip(position, 0, micro_count - 1)
        incoming_gradient = jnp.where(
            section_index == sections - 1, pick_slot(cotangent, slot_index), arrived
        )
        rows_in = pick_slot(kept_rows, slot_index)
        float_cast, inverse_root_mean, normed, pre_act, hidden = inner_section(
            rows_in, gain_row, weight_first
        )
        normed_all = put_slot(normed_all, normed, slot_index, active_flag)
        hidden_gathered = put_slot(hidden_gathered, hidden, slot_index, active_flag)
        grad_rows, grad_pre = backward_section(
            float_cast,
            inverse_root_mean,
            pre_act,
            incoming_gradient,
            gain_row,
            weight_first,
            weight_second,
        )
        grad_all = put_slot(grad_all, grad_pre, slot_index, active_flag)
        upstream_all = put_slot(upstream_all, incoming_gradient, slot_index, active_flag)
        return (grad_rows, normed_all, hidden_gathered, grad_all, upstream_all)

    start_state = (
        empty_rows,
        normed_start,
        hidden_start,
        buffer(inner_width, jnp.bfloat16),
        buffer(model_width, jnp.bfloat16),
    )
    unused, normed_all, hidden_gathered, grad_all, upstream_all = lax.fori_loop(
        0, tick_count, backward_tick, start_state
    )
    tokens = micro_count * row_count
    normed_flat = normed_all.reshape(tokens, model_width)
    hidden_flat = hidden_gathered.reshape(tokens, inner_width)
    grad_flat = grad_all.reshape(tokens, inner_width)
    upstream_flat = upstream_all.reshape(tokens, model_width)
    term_in = jnp.einsum("td,tr->dr", normed_flat, grad_flat, preferred_element_type=jnp.float32)
    term_out = jnp.einsum(
        "tr,td->rd", hidden_flat, upstream_flat, preferred_element_type=jnp.float32
    )
    total_in = lax.psum_scatter(term_in.astype(jnp.bfloat16), "dp", scatter_dimension=0, tiled=True)
    total_out = lax.psum_scatter(
        term_out.astype(jnp.bfloat16), "dp", scatter_dimension=1, tiled=True
    )
    return (total_in[None], total_out[None])


def solution(mesh):
    in_specs = (
        P(None, "dp", None),
        P(None, "dp", None),
        P(),
        P("pipe", None),
        P("pipe", None, None),
        P("pipe", None, None),
    )
    out_specs = (P("pipe", "dp", None), P("pipe", None, "dp"))
    return jax.shard_map(
        per_device, mesh=mesh, in_specs=in_specs, out_specs=out_specs, check_vma=False
    )
```

profile of v0, /device:TPU:31, one launch (start us, length us, event | category | flops | bytes accessed | tf_op | source)
XLA Modules:
  0.0 625.9 jit_solution(13173305586158950125)
XLA Ops:
  9.2 212.7 %while.41 = (s32[]{:T(128)}, bf16[32,8192]{1,0:T(8,128)(2,1)S(1)}, bf16[6,32,8192]{2,1,0:T(8,128)(2,1)}, pred[]{:T(512)}, s32[]{:T(128)}, /*index=5*/s32[6]{0:T(...) while((s32[]{:T(128)}, bf16[32,8192]{1,0:T(8,128)(2,1)S(1)}, ...), condition=%wide.region_2.3_spmd.clone, body=%wide.region_0.2_spmd.clone.sunk | while | flops 540360768 | bytes 25199916 | solution.py:90
  14.1 9.8 %collective-permute-done = bf16[32,8192]{1,0:T(8,128)(2,1)S(1)} collective-permute-done((bf16[32,8192]{1,0:T(8,128)(2,1)S(1)}, bf16[32,8192]{1,0:T(8,128)(2,1)S(1)}, u32[]{:S(2)}, u32[]{:S(2)}) %collective-permute-start) | collective-permute-done | bytes 524320 | tf_op jit(solution)/shard_map/while/body/eval_jaxpr/ppermute | solution.py:12
  26.3 8.9 %fusion.68 = bf16[32,8192]{1,0:T(8,128)(2,1)S(1)} fusion(bf16[512,8192]{1,0:T(8,128)(2,1)} %get-tuple-element.825, bf16[32,8192]{1,0:T(8,128)(2,1)S(1)} %get-tuple-element.761, bf16[8192,512]{1,0:T(8,128)(2,1)} %get-tuple-element.824, f32[8192]{0:T(1024)S(1)} %bitcast.129, f32[32]{0:T(128)S(1)} %add_rsqrt_fusion.4), kind=kOutput, calls=%fused_computation.1.clone.1 | convolution fusion | flops 538787840 | bytes 17858688 | tf_op jit(solution)/shard_map/while/body/eval_jaxpr/dot_general | solution.py:84
  40.1 9.0 %collective-permute-done = bf16[32,8192]{1,0:T(8,128)(2,1)S(1)} collective-permute-done((bf16[32,8192]{1,0:T(8,128)(2,1)S(1)}, bf16[32,8192]{1,0:T(8,128)(2,1)S(1)}, u32[]{:S(2)}, u32[]{:S(2)}) %collective-permute-start) | collective-permute-done | bytes 524320 | tf_op jit(solution)/shard_map/while/body/eval_jaxpr/ppermute | solution.py:12
  51.4 8.9 %fusion.68 = bf16[32,8192]{1,0:T(8,128)(2,1)S(1)} fusion(bf16[512,8192]{1,0:T(8,128)(2,1)} %get-tuple-element.825, bf16[32,8192]{1,0:T(8,128)(2,1)S(1)} %get-tuple-element.761, bf16[8192,512]{1,0:T(8,128)(2,1)} %get-tuple-element.824, f32[8192]{0:T(1024)S(1)} %bitcast.129, f32[32]{0:T(128)S(1)} %add_rsqrt_fusion.4), kind=kOutput, calls=%fused_computation.1.clone.1 | convolution fusion | flops 538787840 | bytes 17858688 | tf_op jit(solution)/shard_map/while/body/eval_jaxpr/dot_general | solution.py:84
  65.2 9.0 %collective-permute-done = bf16[32,8192]{1,0:T(8,128)(2,1)S(1)} collective-permute-done((bf16[32,8192]{1,0:T(8,128)(2,1)S(1)}, bf16[32,8192]{1,0:T(8,128)(2,1)S(1)}, u32[]{:S(2)}, u32[]{:S(2)}) %collective-permute-start) | collective-permute-done | bytes 524320 | tf_op jit(solution)/shard_map/while/body/eval_jaxpr/ppermute | solution.py:12
  76.5 8.9 %fusion.68 = bf16[32,8192]{1,0:T(8,128)(2,1)S(1)} fusion(bf16[512,8192]{1,0:T(8,128)(2,1)} %get-tuple-element.825, bf16[32,8192]{1,0:T(8,128)(2,1)S(1)} %get-tuple-element.761, bf16[8192,512]{1,0:T(8,128)(2,1)} %get-tuple-element.824, f32[8192]{0:T(1024)S(1)} %bitcast.129, f32[32]{0:T(128)S(1)} %add_rsqrt_fusion.4), kind=kOutput, calls=%fused_computation.1.clone.1 | convolution fusion | flops 538787840 | bytes 17858688 | tf_op jit(solution)/shard_map/while/body/eval_jaxpr/dot_general | solution.py:84
  90.4 8.2 %collective-permute-done = bf16[32,8192]{1,0:T(8,128)(2,1)S(1)} collective-permute-done((bf16[32,8192]{1,0:T(8,128)(2,1)S(1)}, bf16[32,8192]{1,0:T(8,128)(2,1)S(1)}, u32[]{:S(2)}, u32[]{:S(2)}) %collective-permute-start) | collective-permute-done | bytes 524320 | tf_op jit(solution)/shard_map/while/body/eval_jaxpr/ppermute | solution.py:12
  100.9 8.9 %fusion.68 = bf16[32,8192]{1,0:T(8,128)(2,1)S(1)} fusion(bf16[512,8192]{1,0:T(8,128)(2,1)} %get-tuple-element.825, bf16[32,8192]{1,0:T(8,128)(2,1)S(1)} %get-tuple-element.761, bf16[8192,512]{1,0:T(8,128)(2,1)} %get-tuple-element.824, f32[8192]{0:T(1024)S(1)} %bitcast.129, f32[32]{0:T(128)S(1)} %add_rsqrt_fusion.4), kind=kOutput, calls=%fused_computation.1.clone.1 | convolution fusion | flops 538787840 | bytes 17858688 | tf_op jit(solution)/shard_map/while/body/eval_jaxpr/dot_general | solution.py:84
  114.7 7.3 %collective-permute-done = bf16[32,8192]{1,0:T(8,128)(2,1)S(1)} collective-permute-done((bf16[32,8192]{1,0:T(8,128)(2,1)S(1)}, bf16[32,8192]{1,0:T(8,128)(2,1)S(1)}, u32[]{:S(2)}, u32[]{:S(2)}) %collective-permute-start) | collective-permute-done | bytes 524320 | tf_op jit(solution)/shard_map/while/body/eval_jaxpr/ppermute | solution.py:12
  124.3 8.9 %fusion.68 = bf16[32,8192]{1,0:T(8,128)(2,1)S(1)} fusion(bf16[512,8192]{1,0:T(8,128)(2,1)} %get-tuple-element.825, bf16[32,8192]{1,0:T(8,128)(2,1)S(1)} %get-tuple-element.761, bf16[8192,512]{1,0:T(8,128)(2,1)} %get-tuple-element.824, f32[8192]{0:T(1024)S(1)} %bitcast.129, f32[32]{0:T(128)S(1)} %add_rsqrt_fusion.4), kind=kOutput, calls=%fused_computation.1.clone.1 | convolution fusion | flops 538787840 | bytes 17858688 | tf_op jit(solution)/shard_map/while/body/eval_jaxpr/dot_general | solution.py:84
  138.1 6.5 %collective-permute-done = bf16[32,8192]{1,0:T(8,128)(2,1)S(1)} collective-permute-done((bf16[32,8192]{1,0:T(8,128)(2,1)S(1)}, bf16[32,8192]{1,0:T(8,128)(2,1)S(1)}, u32[]{:S(2)}, u32[]{:S(2)}) %collective-permute-start) | collective-permute-done | bytes 524320 | tf_op jit(solution)/shard_map/while/body/eval_jaxpr/ppermute | solution.py:12
  147.0 8.9 %fusion.68 = bf16[32,8192]{1,0:T(8,128)(2,1)S(1)} fusion(bf16[512,8192]{1,0:T(8,128)(2,1)} %get-tuple-element.825, bf16[32,8192]{1,0:T(8,128)(2,1)S(1)} %get-tuple-element.761, bf16[8192,512]{1,0:T(8,128)(2,1)} %get-tuple-element.824, f32[8192]{0:T(1024)S(1)} %bitcast.129, f32[32]{0:T(128)S(1)} %add_rsqrt_fusion.4), kind=kOutput, calls=%fused_computation.1.clone.1 | convolution fusion | flops 538787840 | bytes 17858688 | tf_op jit(solution)/shard_map/while/body/eval_jaxpr/dot_general | solution.py:84
  160.9 5.6 collective-permute-done
  168.8 8.9 %fusion.68 = bf16[32,8192]{1,0:T(8,128)(2,1)S(1)} fusion(bf16[512,8192]{1,0:T(8,128)(2,1)} %get-tuple-element.825, bf16[32,8192]{1,0:T(8,128)(2,1)S(1)} %get-tuple-element.761, bf16[8192,512]{1,0:T(8,128)(2,1)} %get-tuple-element.824, f32[8192]{0:T(1024)S(1)} %bitcast.129, f32[32]{0:T(128)S(1)} %add_rsqrt_fusion.4), kind=kOutput, calls=%fused_computation.1.clone.1 | convolution fusion | flops 538787840 | bytes 17858688 | tf_op jit(solution)/shard_map/while/body/eval_jaxpr/dot_general | solution.py:84
  182.7 6.0 collective-permute-done
  190.9 8.9 %fusion.68 = bf16[32,8192]{1,0:T(8,128)(2,1)S(1)} fusion(bf16[512,8192]{1,0:T(8,128)(2,1)} %get-tuple-element.825, bf16[32,8192]{1,0:T(8,128)(2,1)S(1)} %get-tuple-element.761, bf16[8192,512]{1,0:T(8,128)(2,1)} %get-tuple-element.824, f32[8192]{0:T(1024)S(1)} %bitcast.129, f32[32]{0:T(128)S(1)} %add_rsqrt_fusion.4), kind=kOutput, calls=%fused_computation.1.clone.1 | convolution fusion | flops 538787840 | bytes 17858688 | tf_op jit(solution)/shard_map/while/body/eval_jaxpr/dot_general | solution.py:84
  204.8 6.0 collective-permute-done
  213.0 8.9 %fusion.68 = bf16[32,8192]{1,0:T(8,128)(2,1)S(1)} fusion(bf16[512,8192]{1,0:T(8,128)(2,1)} %get-tuple-element.825, bf16[32,8192]{1,0:T(8,128)(2,1)S(1)} %get-tuple-element.761, bf16[8192,512]{1,0:T(8,128)(2,1)} %get-tuple-element.824, f32[8192]{0:T(1024)S(1)} %bitcast.129, f32[32]{0:T(128)S(1)} %add_rsqrt_fusion.4), kind=kOutput, calls=%fused_computation.1.clone.1 | convolution fusion | flops 538787840 | bytes 17858688 | tf_op jit(solution)/shard_map/while/body/eval_jaxpr/dot_general | solution.py:84
  226.1 193.1 %while.42 = (s32[]{:T(128)}, bf16[32,8192]{1,0:T(8,128)(2,1)S(1)}, bf16[6,32,8192]{2,1,0:T(8,128)(2,1)}, bf16[6,32,512]{2,1,0:T(8,128)(2,1)S(1)}, bf16[6,32,512]...) while((s32[]{:T(128)}, bf16[32,8192]{1,0:T(8,128)(2,1)S(1)}, ...), condition=%wide.region_6.7_spmd.clone, body=%wide.region_3.6_spmd.clone.sunk | while | flops 812908544 | bytes 98603120 | solution.py:131
  226.2 4.3 collective-permute-start.1
  231.8 2.6 fusion.75
  234.4 5.3 bitcast_dynamic-update-slice_fusion.9
  244.6 3.7 fusion.76
  253.0 2.6 fusion.75
  255.6 5.3 bitcast_dynamic-update-slice_fusion.9
  265.8 3.7 fusion.76
  276.8 5.3 bitcast_dynamic-update-slice_fusion.9
  284.4 2.6 bitcast_dynamic-update-slice_fusion.11
  287.0 3.7 fusion.76
  298.0 5.3 bitcast_dynamic-update-slice_fusion.9
  305.6 2.6 bitcast_dynamic-update-slice_fusion.11
  308.2 3.7 fusion.76
  319.2 5.3 bitcast_dynamic-update-slice_fusion.9
  329.4 3.7 fusion.76
  340.4 5.3 bitcast_dynamic-update-slice_fusion.9
  348.0 2.6 bitcast_dynamic-update-slice_fusion.11
  350.6 3.7 fusion.76
  361.6 5.3 bitcast_dynamic-update-slice_fusion.9
  371.8 3.7 fusion.76
  382.8 5.3 bitcast_dynamic-update-slice_fusion.9
  393.0 3.7 fusion.76
  403.9 5.3 bitcast_dynamic-update-slice_fusion.9
  414.1 3.7 fusion.76
  419.2 7.6 %bitcast_convert_fusion.1 = bf16[8192,512]{1,0:T(8,128)(2,1)} fusion(bf16[6,32,8192]{2,1,0:T(8,128)(2,1)} %get-tuple-element.481, bf16[6,32,512]{2,1,0:T(8,128)(2,1)S(1)} %get-tuple-element.482), kind=kOutput, calls=%fused_computation.62 | convolution fusion | flops 1614807040 | bytes 11730944 | tf_op jit(solution)/shard_map/td,tr->dr/dot_general | solution.py:139
  428.7 5.6 bitcast_convert_fusion
  434.4 93.8 %reduce-scatter.3.cloned.1.call-done = bf16[1024,512]{1,0:T(8,128)(2,1)} async-done(((bf16[8192,512]{1,0:T(8,128)(2,1)}), bf16[1024,512]{1,0:T(8,128)(2,1)}) %reduce-scatter.3.cloned.1.call-update) | async-done | bytes 1048592 | tf_op jit(solution)/shard_map/reduce_scatter | solution.py:143
  528.2 90.9 %reduce-scatter.5.cloned.1.call-done = bf16[512,1024]{1,0:T(8,128)(2,1)} async-done(((bf16[512,8192]{1,0:T(8,128)(2,1)}), bf16[512,1024]{1,0:T(8,128)(2,1)}) %reduce-scatter.5.cloned.1.call-update) | async-done | bytes 1048592 | tf_op jit(solution)/shard_map/reduce_scatter | solution.py:144
  (236 shorter events, 149.6 us)
Async XLA Ops:
  7.2 2.1 copy-start.1
  7.2 521.0 %reduce-scatter.3.cloned.1.call-start = ((), (), s32[]{:S(2)}) async-start(), calls=%async_computation.2 | async-start | bytes 9437184 | tf_op jit(solution)/shard_map/reduce_scatter | solution.py:143
  9.3 14.7 %collective-permute-start = (bf16[32,8192]{1,0:T(8,128)(2,1)S(1)}, bf16[32,8192]{1,0:T(8,128)(2,1)S(1)}, u32[]{:S(2)}, u32[]{:S(2)}) collective-permute-start(bf16[32,8192]{1,0:T(8,128)(2,1)S(1)} %broadcast_select_fusion.4), channel_id=1, source_target_pairs={{0,8},{8,16},{16,24},{1,9},{9,17},{17,25},{2,10},{10,18},{18,26},{... | collective-permute-start | bytes 1572872 | tf_op jit(solution)/shard_map/while/body/eval_jaxpr/ppermute | solution.py:12
  35.3 13.8 %collective-permute-start = (bf16[32,8192]{1,0:T(8,128)(2,1)S(1)}, bf16[32,8192]{1,0:T(8,128)(2,1)S(1)}, u32[]{:S(2)}, u32[]{:S(2)}) collective-permute-start(bf16[32,8192]{1,0:T(8,128)(2,1)S(1)} %broadcast_select_fusion.4), channel_id=1, source_target_pairs={{0,8},{8,16},{16,24},{1,9},{9,17},{17,25},{2,10},{10,18},{18,26},{... | collective-permute-start | bytes 1572872 | tf_op jit(solution)/shard_map/while/body/eval_jaxpr/ppermute | solution.py:12
  60.4 13.9 %collective-permute-start = (bf16[32,8192]{1,0:T(8,128)(2,1)S(1)}, bf16[32,8192]{1,0:T(8,128)(2,1)S(1)}, u32[]{:S(2)}, u32[]{:S(2)}) collective-permute-start(bf16[32,8192]{1,0:T(8,128)(2,1)S(1)} %broadcast_select_fusion.4), channel_id=1, source_target_pairs={{0,8},{8,16},{16,24},{1,9},{9,17},{17,25},{2,10},{10,18},{18,26},{... | collective-permute-start | bytes 1572872 | tf_op jit(solution)/shard_map/while/body/eval_jaxpr/ppermute | solution.py:12
  85.5 13.0 %collective-permute-start = (bf16[32,8192]{1,0:T(8,128)(2,1)S(1)}, bf16[32,8192]{1,0:T(8,128)(2,1)S(1)}, u32[]{:S(2)}, u32[]{:S(2)}) collective-permute-start(bf16[32,8192]{1,0:T(8,128)(2,1)S(1)} %broadcast_select_fusion.4), channel_id=1, source_target_pairs={{0,8},{8,16},{16,24},{1,9},{9,17},{17,25},{2,10},{10,18},{18,26},{... | collective-permute-start | bytes 1572872 | tf_op jit(solution)/shard_map/while/body/eval_jaxpr/ppermute | solution.py:12
  109.8 12.2 %collective-permute-start = (bf16[32,8192]{1,0:T(8,128)(2,1)S(1)}, bf16[32,8192]{1,0:T(8,128)(2,1)S(1)}, u32[]{:S(2)}, u32[]{:S(2)}) collective-permute-start(bf16[32,8192]{1,0:T(8,128)(2,1)S(1)} %broadcast_select_fusion.4), channel_id=1, source_target_pairs={{0,8},{8,16},{16,24},{1,9},{9,17},{17,25},{2,10},{10,18},{18,26},{... | collective-permute-start | bytes 1572872 | tf_op jit(solution)/shard_map/while/body/eval_jaxpr/ppermute | solution.py:12
  133.3 11.4 %collective-permute-start = (bf16[32,8192]{1,0:T(8,128)(2,1)S(1)}, bf16[32,8192]{1,0:T(8,128)(2,1)S(1)}, u32[]{:S(2)}, u32[]{:S(2)}) collective-permute-start(bf16[32,8192]{1,0:T(8,128)(2,1)S(1)} %broadcast_select_fusion.4), channel_id=1, source_target_pairs={{0,8},{8,16},{16,24},{1,9},{9,17},{17,25},{2,10},{10,18},{18,26},{... | collective-permute-start | bytes 1572872 | tf_op jit(solution)/shard_map/while/body/eval_jaxpr/ppermute | solution.py:12
  156.0 10.5 %collective-permute-start = (bf16[32,8192]{1,0:T(8,128)(2,1)S(1)}, bf16[32,8192]{1,0:T(8,128)(2,1)S(1)}, u32[]{:S(2)}, u32[]{:S(2)}) collective-permute-start(bf16[32,8192]{1,0:T(8,128)(2,1)S(1)} %broadcast_select_fusion.4), channel_id=1, source_target_pairs={{0,8},{8,16},{16,24},{1,9},{9,17},{17,25},{2,10},{10,18},{18,26},{... | collective-permute-start | bytes 1572872 | tf_op jit(solution)/shard_map/while/body/eval_jaxpr/ppermute | solution.py:12
  177.8 10.8 %collective-permute-start = (bf16[32,8192]{1,0:T(8,128)(2,1)S(1)}, bf16[32,8192]{1,0:T(8,128)(2,1)S(1)}, u32[]{:S(2)}, u32[]{:S(2)}) collective-permute-start(bf16[32,8192]{1,0:T(8,128)(2,1)S(1)} %broadcast_select_fusion.4), channel_id=1, source_target_pairs={{0,8},{8,16},{16,24},{1,9},{9,17},{17,25},{2,10},{10,18},{18,26},{... | collective-permute-start | bytes 1572872 | tf_op jit(solution)/shard_map/while/body/eval_jaxpr/ppermute | solution.py:12
  199.9 10.8 %collective-permute-start = (bf16[32,8192]{1,0:T(8,128)(2,1)S(1)}, bf16[32,8192]{1,0:T(8,128)(2,1)S(1)}, u32[]{:S(2)}, u32[]{:S(2)}) collective-permute-start(bf16[32,8192]{1,0:T(8,128)(2,1)S(1)} %broadcast_select_fusion.4), channel_id=1, source_target_pairs={{0,8},{8,16},{16,24},{1,9},{9,17},{17,25},{2,10},{10,18},{18,26},{... | collective-permute-start | bytes 1572872 | tf_op jit(solution)/shard_map/while/body/eval_jaxpr/ppermute | solution.py:12
  226.2 13.5 %collective-permute-start.1 = (bf16[32,8192]{1,0:T(8,128)(2,1)S(1)}, bf16[32,8192]{1,0:T(8,128)(2,1)S(1)}, u32[]{:S(2)}, u32[]{:S(2)}) collective-permute-start(bf16[32,8192]{1,0:T(8,128)(2,1)S(1)} %broadcast_select_fusion.5), channel_id=1, source_target_pairs={{8,0},{16,8},{24,16},{9,1},{17,9},{25,17},{10,2},{18,10},{26,18},{... | collective-permute-start | bytes 1572872 | tf_op jit(solution)/shard_map/while/body/eval_jaxpr/ppermute | solution.py:12
  231.8 12.8 %slice-start = ((s8[8388608]{0:T(1024)(128)(4,1)}), s8[4194304]{0:T(1024)(128)(4,1)S(1)}, s32[]{:S(2)}) async-start(s8[8388608]{0:T(1024)(128)(4,1)} %bitcast.126), calls=%async_computation.4 | async-start | bytes 8388608 | tf_op jit(solution)/shard_map/while
  234.4 7.6 %copy-start = (bf16[512,8192]{1,0:T(8,128)(2,1)S(1)}, bf16[512,8192]{1,0:T(8,128)(2,1)}, u32[]{:S(2)}) copy-start(bf16[512,8192]{1,0:T(8,128)(2,1)} %get-tuple-element.874) | copy-start | bytes 25165828 | tf_op jit(solution)/shard_map/while
  234.4 10.2 %slice-start.1 = ((s8[8388608]{0:T(1024)(128)(4,1)}), s8[4194304]{0:T(1024)(128)(4,1)S(1)}, s32[]{:S(2)}) async-start(s8[8388608]{0:T(1024)(128)(4,1)} %bitcast.126), calls=%async_computation.5 | async-start | bytes 8388608 | tf_op jit(solution)/shard_map/while
  249.8 11.2 %collective-permute-start.1 = (bf16[32,8192]{1,0:T(8,128)(2,1)S(1)}, bf16[32,8192]{1,0:T(8,128)(2,1)S(1)}, u32[]{:S(2)}, u32[]{:S(2)}) collective-permute-start(bf16[32,8192]{1,0:T(8,128)(2,1)S(1)} %broadcast_select_fusion.5), channel_id=1, source_target_pairs={{8,0},{16,8},{24,16},{9,1},{17,9},{25,17},{10,2},{18,10},{26,18},{... | collective-permute-start | bytes 1572872 | tf_op jit(solution)/shard_map/while/body/eval_jaxpr/ppermute | solution.py:12
  253.0 12.8 %slice-start = ((s8[8388608]{0:T(1024)(128)(4,1)}), s8[4194304]{0:T(1024)(128)(4,1)S(1)}, s32[]{:S(2)}) async-start(s8[8388608]{0:T(1024)(128)(4,1)} %bitcast.126), calls=%async_computation.4 | async-start | bytes 8388608 | tf_op jit(solution)/shard_map/while
  255.6 7.6 %copy-start = (bf16[512,8192]{1,0:T(8,128)(2,1)S(1)}, bf16[512,8192]{1,0:T(8,128)(2,1)}, u32[]{:S(2)}) copy-start(bf16[512,8192]{1,0:T(8,128)(2,1)} %get-tuple-element.874) | copy-start | bytes 25165828 | tf_op jit(solution)/shard_map/while
  255.6 10.2 %slice-start.1 = ((s8[8388608]{0:T(1024)(128)(4,1)}), s8[4194304]{0:T(1024)(128)(4,1)S(1)}, s32[]{:S(2)}) async-start(s8[8388608]{0:T(1024)(128)(4,1)} %bitcast.126), calls=%async_computation.5 | async-start | bytes 8388608 | tf_op jit(solution)/shard_map/while
  271.0 11.1 %collective-permute-start.1 = (bf16[32,8192]{1,0:T(8,128)(2,1)S(1)}, bf16[32,8192]{1,0:T(8,128)(2,1)S(1)}, u32[]{:S(2)}, u32[]{:S(2)}) collective-permute-start(bf16[32,8192]{1,0:T(8,128)(2,1)S(1)} %broadcast_select_fusion.5), channel_id=1, source_target_pairs={{8,0},{16,8},{24,16},{9,1},{17,9},{25,17},{10,2},{18,10},{26,18},{... | collective-permute-start | bytes 1572872 | tf_op jit(solution)/shard_map/while/body/eval_jaxpr/ppermute | solution.py:12
  274.2 12.8 %slice-start = ((s8[8388608]{0:T(1024)(128)(4,1)}), s8[4194304]{0:T(1024)(128)(4,1)S(1)}, s32[]{:S(2)}) async-start(s8[8388608]{0:T(1024)(128)(4,1)} %bitcast.126), calls=%async_computation.4 | async-start | bytes 8388608 | tf_op jit(solution)/shard_map/while
  276.8 7.6 %copy-start = (bf16[512,8192]{1,0:T(8,128)(2,1)S(1)}, bf16[512,8192]{1,0:T(8,128)(2,1)}, u32[]{:S(2)}) copy-start(bf16[512,8192]{1,0:T(8,128)(2,1)} %get-tuple-element.874) | copy-start | bytes 25165828 | tf_op jit(solution)/shard_map/while
  276.8 10.2 %slice-start.1 = ((s8[8388608]{0:T(1024)(128)(4,1)}), s8[4194304]{0:T(1024)(128)(4,1)S(1)}, s32[]{:S(2)}) async-start(s8[8388608]{0:T(1024)(128)(4,1)} %bitcast.126), calls=%async_computation.5 | async-start | bytes 8388608 | tf_op jit(solution)/shard_map/while
  292.1 11.2 %collective-permute-start.1 = (bf16[32,8192]{1,0:T(8,128)(2,1)S(1)}, bf16[32,8192]{1,0:T(8,128)(2,1)S(1)}, u32[]{:S(2)}, u32[]{:S(2)}) collective-permute-start(bf16[32,8192]{1,0:T(8,128)(2,1)S(1)} %broadcast_select_fusion.5), channel_id=1, source_target_pairs={{8,0},{16,8},{24,16},{9,1},{17,9},{25,17},{10,2},{18,10},{26,18},{... | collective-permute-start | bytes 1572872 | tf_op jit(solution)/shard_map/while/body/eval_jaxpr/ppermute | solution.py:12
  295.4 12.8 %slice-start = ((s8[8388608]{0:T(1024)(128)(4,1)}), s8[4194304]{0:T(1024)(128)(4,1)S(1)}, s32[]{:S(2)}) async-start(s8[8388608]{0:T(1024)(128)(4,1)} %bitcast.126), calls=%async_computation.4 | async-start | bytes 8388608 | tf_op jit(solution)/shard_map/while
  298.0 7.6 %copy-start = (bf16[512,8192]{1,0:T(8,128)(2,1)S(1)}, bf16[512,8192]{1,0:T(8,128)(2,1)}, u32[]{:S(2)}) copy-start(bf16[512,8192]{1,0:T(8,128)(2,1)} %get-tuple-element.874) | copy-start | bytes 25165828 | tf_op jit(solution)/shard_map/while
  298.0 10.2 %slice-start.1 = ((s8[8388608]{0:T(1024)(128)(4,1)}), s8[4194304]{0:T(1024)(128)(4,1)S(1)}, s32[]{:S(2)}) async-start(s8[8388608]{0:T(1024)(128)(4,1)} %bitcast.126), calls=%async_computation.5 | async-start | bytes 8388608 | tf_op jit(solution)/shard_map/while
  313.4 11.1 %collective-permute-start.1 = (bf16[32,8192]{1,0:T(8,128)(2,1)S(1)}, bf16[32,8192]{1,0:T(8,128)(2,1)S(1)}, u32[]{:S(2)}, u32[]{:S(2)}) collective-permute-start(bf16[32,8192]{1,0:T(8,128)(2,1)S(1)} %broadcast_select_fusion.5), channel_id=1, source_target_pairs={{8,0},{16,8},{24,16},{9,1},{17,9},{25,17},{10,2},{18,10},{26,18},{... | collective-permute-start | bytes 1572872 | tf_op jit(solution)/shard_map/while/body/eval_jaxpr/ppermute | solution.py:12
  316.6 12.8 %slice-start = ((s8[8388608]{0:T(1024)(128)(4,1)}), s8[4194304]{0:T(1024)(128)(4,1)S(1)}, s32[]{:S(2)}) async-start(s8[8388608]{0:T(1024)(128)(4,1)} %bitcast.126), calls=%async_computation.4 | async-start | bytes 8388608 | tf_op jit(solution)/shard_map/while
  319.2 7.6 %copy-start = (bf16[512,8192]{1,0:T(8,128)(2,1)S(1)}, bf16[512,8192]{1,0:T(8,128)(2,1)}, u32[]{:S(2)}) copy-start(bf16[512,8192]{1,0:T(8,128)(2,1)} %get-tuple-element.874) | copy-start | bytes 25165828 | tf_op jit(solution)/shard_map/while
  319.2 10.2 %slice-start.1 = ((s8[8388608]{0:T(1024)(128)(4,1)}), s8[4194304]{0:T(1024)(128)(4,1)S(1)}, s32[]{:S(2)}) async-start(s8[8388608]{0:T(1024)(128)(4,1)} %bitcast.126), calls=%async_computation.5 | async-start | bytes 8388608 | tf_op jit(solution)/shard_map/while
  334.6 11.1 %collective-permute-start.1 = (bf16[32,8192]{1,0:T(8,128)(2,1)S(1)}, bf16[32,8192]{1,0:T(8,128)(2,1)S(1)}, u32[]{:S(2)}, u32[]{:S(2)}) collective-permute-start(bf16[32,8192]{1,0:T(8,128)(2,1)S(1)} %broadcast_select_fusion.5), channel_id=1, source_target_pairs={{8,0},{16,8},{24,16},{9,1},{17,9},{25,17},{10,2},{18,10},{26,18},{... | collective-permute-start | bytes 1572872 | tf_op jit(solution)/shard_map/while/body/eval_jaxpr/ppermute | solution.py:12
  337.8 12.8 %slice-start = ((s8[8388608]{0:T(1024)(128)(4,1)}), s8[4194304]{0:T(1024)(128)(4,1)S(1)}, s32[]{:S(2)}) async-start(s8[8388608]{0:T(1024)(128)(4,1)} %bitcast.126), calls=%async_computation.4 | async-start | bytes 8388608 | tf_op jit(solution)/shard_map/while
  340.4 7.6 %copy-start = (bf16[512,8192]{1,0:T(8,128)(2,1)S(1)}, bf16[512,8192]{1,0:T(8,128)(2,1)}, u32[]{:S(2)}) copy-start(bf16[512,8192]{1,0:T(8,128)(2,1)} %get-tuple-element.874) | copy-start | bytes 25165828 | tf_op jit(solution)/shard_map/while
  340.4 10.2 %slice-start.1 = ((s8[8388608]{0:T(1024)(128)(4,1)}), s8[4194304]{0:T(1024)(128)(4,1)S(1)}, s32[]{:S(2)}) async-start(s8[8388608]{0:T(1024)(128)(4,1)} %bitcast.126), calls=%async_computation.5 | async-start | bytes 8388608 | tf_op jit(solution)/shard_map/while
  355.8 11.2 %collective-permute-start.1 = (bf16[32,8192]{1,0:T(8,128)(2,1)S(1)}, bf16[32,8192]{1,0:T(8,128)(2,1)S(1)}, u32[]{:S(2)}, u32[]{:S(2)}) collective-permute-start(bf16[32,8192]{1,0:T(8,128)(2,1)S(1)} %broadcast_select_fusion.5), channel_id=1, source_target_pairs={{8,0},{16,8},{24,16},{9,1},{17,9},{25,17},{10,2},{18,10},{26,18},{... | collective-permute-start | bytes 1572872 | tf_op jit(solution)/shard_map/while/body/eval_jaxpr/ppermute | solution.py:12
  359.0 12.8 %slice-start = ((s8[8388608]{0:T(1024)(128)(4,1)}), s8[4194304]{0:T(1024)(128)(4,1)S(1)}, s32[]{:S(2)}) async-start(s8[8388608]{0:T(1024)(128)(4,1)} %bitcast.126), calls=%async_computation.4 | async-start | bytes 8388608 | tf_op jit(solution)/shard_map/while
  361.6 7.6 %copy-start = (bf16[512,8192]{1,0:T(8,128)(2,1)S(1)}, bf16[512,8192]{1,0:T(8,128)(2,1)}, u32[]{:S(2)}) copy-start(bf16[512,8192]{1,0:T(8,128)(2,1)} %get-tuple-element.874) | copy-start | bytes 25165828 | tf_op jit(solution)/shard_map/while
  361.6 10.2 %slice-start.1 = ((s8[8388608]{0:T(1024)(128)(4,1)}), s8[4194304]{0:T(1024)(128)(4,1)S(1)}, s32[]{:S(2)}) async-start(s8[8388608]{0:T(1024)(128)(4,1)} %bitcast.126), calls=%async_computation.5 | async-start | bytes 8388608 | tf_op jit(solution)/shard_map/while
  377.0 11.1 %collective-permute-start.1 = (bf16[32,8192]{1,0:T(8,128)(2,1)S(1)}, bf16[32,8192]{1,0:T(8,128)(2,1)S(1)}, u32[]{:S(2)}, u32[]{:S(2)}) collective-permute-start(bf16[32,8192]{1,0:T(8,128)(2,1)S(1)} %broadcast_select_fusion.5), channel_id=1, source_target_pairs={{8,0},{16,8},{24,16},{9,1},{17,9},{25,17},{10,2},{18,10},{26,18},{... | collective-permute-start | bytes 1572872 | tf_op jit(solution)/shard_map/while/body/eval_jaxpr/ppermute | solution.py:12
  380.2 12.8 %slice-start = ((s8[8388608]{0:T(1024)(128)(4,1)}), s8[4194304]{0:T(1024)(128)(4,1)S(1)}, s32[]{:S(2)}) async-start(s8[8388608]{0:T(1024)(128)(4,1)} %bitcast.126), calls=%async_computation.4 | async-start | bytes 8388608 | tf_op jit(solution)/shard_map/while
  382.8 7.6 %copy-start = (bf16[512,8192]{1,0:T(8,128)(2,1)S(1)}, bf16[512,8192]{1,0:T(8,128)(2,1)}, u32[]{:S(2)}) copy-start(bf16[512,8192]{1,0:T(8,128)(2,1)} %get-tuple-element.874) | copy-start | bytes 25165828 | tf_op jit(solution)/shard_map/while
  382.8 10.2 %slice-start.1 = ((s8[8388608]{0:T(1024)(128)(4,1)}), s8[4194304]{0:T(1024)(128)(4,1)S(1)}, s32[]{:S(2)}) async-start(s8[8388608]{0:T(1024)(128)(4,1)} %bitcast.126), calls=%async_computation.5 | async-start | bytes 8388608 | tf_op jit(solution)/shard_map/while
  398.1 11.1 %collective-permute-start.1 = (bf16[32,8192]{1,0:T(8,128)(2,1)S(1)}, bf16[32,8192]{1,0:T(8,128)(2,1)S(1)}, u32[]{:S(2)}, u32[]{:S(2)}) collective-permute-start(bf16[32,8192]{1,0:T(8,128)(2,1)S(1)} %broadcast_select_fusion.5), channel_id=1, source_target_pairs={{8,0},{16,8},{24,16},{9,1},{17,9},{25,17},{10,2},{18,10},{26,18},{... | collective-permute-start | bytes 1572872 | tf_op jit(solution)/shard_map/while/body/eval_jaxpr/ppermute | solution.py:12
  401.4 12.8 %slice-start = ((s8[8388608]{0:T(1024)(128)(4,1)}), s8[4194304]{0:T(1024)(128)(4,1)S(1)}, s32[]{:S(2)}) async-start(s8[8388608]{0:T(1024)(128)(4,1)} %bitcast.126), calls=%async_computation.4 | async-start | bytes 8388608 | tf_op jit(solution)/shard_map/while
  403.9 7.6 %copy-start = (bf16[512,8192]{1,0:T(8,128)(2,1)S(1)}, bf16[512,8192]{1,0:T(8,128)(2,1)}, u32[]{:S(2)}) copy-start(bf16[512,8192]{1,0:T(8,128)(2,1)} %get-tuple-element.874) | copy-start | bytes 25165828 | tf_op jit(solution)/shard_map/while
  403.9 10.2 %slice-start.1 = ((s8[8388608]{0:T(1024)(128)(4,1)}), s8[4194304]{0:T(1024)(128)(4,1)S(1)}, s32[]{:S(2)}) async-start(s8[8388608]{0:T(1024)(128)(4,1)} %bitcast.126), calls=%async_computation.5 | async-start | bytes 8388608 | tf_op jit(solution)/shard_map/while
  426.8 192.2 %reduce-scatter.5.cloned.1.call-start = ((), (), s32[]{:S(2)}) async-start(), calls=%async_computation.3 | async-start | bytes 9437184 | tf_op jit(solution)/shard_map/reduce_scatter | solution.py:144
  (2 other events, 4.0 us)
Sparse Core Ops, SparseCore 0:
  427.0 101.1 reduce-scatter.2
  531.1 87.9 reduce-scatter.4
where the time goes:
time: 633 us; the launch traced here: 626 us
  waiting for transfers between devices  252 us (40%)
  matrix products  198 us (31%)
  other arithmetic  88.7 us (14%)
  starting transfers between devices  31.4 us (5%)
  local copies, waits for them, and re-layouts  23.4 us (4%)
  loops' own time  18.5 us (3%)
  between operations  14.1 us (2%)
    reduce_scatter x1, waiting for transfers between devices, per_device(): lax.psum_scatter(term_in.astype(jnp.bfloat16), 'dp', scatter_dimension=0,...  93.8 us
    reduce_scatter x1, waiting for transfers between devices, per_device(): lax.psum_scatter(term_out.astype(jnp.bfloat16), 'dp', scatter_dimension=1...  90.9 us
    dot_general x9, matrix products, forward_tick(): jnp.dot(hidden, weight_second, preferred_element_type=jnp.float32)  80.2 us
    ppermute x18, waiting for transfers between devices, passed_along(): return lax.ppermute(value, axis, pairs)  67.4 us
    dynamic_update_slice x27, other arithmetic, put_slot(): lax.dynamic_update_index_in_dim(buffer, jnp.where(active_flag, new_value,...  61.9 us
    dot_general x9, matrix products, inner_section(): pre_act = jnp.dot(normed, weight_first, preferred_element_type=jnp.float32)  47.8 us
    dot_general x9, matrix products, backward_section(): jnp.einsum('tr,dr->td', grad_pre, weight_first, preferred_element_type=jn...  33.3 us
    ppermute x18, starting transfers between devices, passed_along(): return lax.ppermute(value, axis, pairs)  31.3 us
  transfers between devices with their start and end apart: 20, of which 11 were waited for; matrix products, arithmetic and copies ran while one was open for 16% of the time, Pallas kernels for 0%

commit v1 on v0

v1 whole, which is shorter than its diff:
```python
import functools

import jax
import jax.numpy as jnp
from jax import lax
from jax.experimental import pallas as pl
from jax.experimental.pallas import tpu as pltpu
from jax.sharding import PartitionSpec as P

EPSILON = 1e-05
MESH = pl.DeviceIdType.MESH
CHUNK = 1024
UNROLL = 2


def landed(ref, sem):
    pltpu.make_async_copy(ref, ref, sem).wait()


def train_kernel(
    sections,
    peers,
    rows_hbm,
    cot_hbm,
    gain,
    w_in,
    w_out,
    normed_all,
    up_all,
    hidden_all,
    grad_all,
    xbuf,
    ubuf,
    xsend,
    usend,
    normed,
    back,
    pre_kept,
    hidden_kept,
    grad_kept,
    inv_kept,
    x_recv,
    u_recv,
    x_sent,
    u_sent,
    n_sems,
    p_sems,
    h_sems,
    g_sems,
):
    stage = lax.axis_index("pipe")
    me = lax.axis_index("dp")
    last = sections - 1
    micro, rows, width = xbuf.shape
    share = width // peers
    chunk = min(CHUNK, width)
    chunks = width // chunk

    barrier = pltpu.get_barrier_semaphore()
    for j in range(1, peers):
        pl.semaphore_signal(
            barrier, inc=1, device_id={"dp": lax.rem(me + j, peers)}, device_id_type=MESH
        )

    @pl.when(stage < last)
    def _():
        pl.semaphore_signal(barrier, inc=1, device_id={"pipe": stage + 1}, device_id_type=MESH)

    @pl.when(stage > 0)
    def _():
        pl.semaphore_signal(barrier, inc=1, device_id={"pipe": stage - 1}, device_id_type=MESH)

    pl.semaphore_wait(
        barrier, peers - 1 + jnp.minimum(stage, 1) + jnp.minimum(last - stage, 1)
    )

    @pl.when(stage == 0)
    def _():
        for m in range(micro):
            pltpu.make_async_copy(rows_hbm.at[m], xbuf.at[m], x_recv.at[m]).start()

    @pl.when(stage == last)
    def _():
        for m in range(micro):
            pltpu.make_async_copy(cot_hbm.at[m], ubuf.at[m], u_recv.at[m]).start()

    def cols(c):
        return pl.ds(pl.multiple_of(c * chunk, chunk), chunk)

    def spread_columns(source, target, sems, m):
        for j in range(1, peers):
            peer = lax.rem(me + j, peers)
            pltpu.make_async_remote_copy(
                src_ref=source.at[m, :, pl.ds(pl.multiple_of(peer * share, share), share)],
                dst_ref=target.at[me, m],
                send_sem=sems.at[0],
                recv_sem=sems.at[1],
                device_id={"dp": peer},
                device_id_type=MESH,
            ).start()
        pltpu.make_async_copy(
            source.at[m, :, pl.ds(pl.multiple_of(me * share, share), share)],
            target.at[me, m],
            sems.at[1],
        ).start()

    def spread_whole(source, target, sems, m):
        for j in range(1, peers):
            pltpu.make_async_remote_copy(
                src_ref=source.at[m],
                dst_ref=target.at[me, m],
                send_sem=sems.at[0],
                recv_sem=sems.at[1],
                device_id={"dp": lax.rem(me + j, peers)},
                device_id_type=MESH,
            ).start()
        pltpu.make_async_copy(source.at[m], target.at[me, m], sems.at[1]).start()

    def pass_on(source, target, send, recv, m, to):
        return pltpu.make_async_remote_copy(
            src_ref=source.at[m],
            dst_ref=target.at[m],
            send_sem=send.at[m],
            recv_sem=recv.at[m],
            device_id={"pipe": to},
            device_id_type=MESH,
        )

    def forward(m):
        landed(xbuf.at[m], x_recv.at[m])

        def square(c, total):
            x = xbuf[m, :, cols(c)].astype(jnp.float32)
            return total + jnp.sum(x * x, axis=-1, keepdims=True)

        total = lax.fori_loop(
            0, chunks, square, jnp.zeros((rows, 1), jnp.float32), unroll=UNROLL
        )
        inverse = lax.rsqrt(total / width + EPSILON)
        inv_kept[m] = jnp.broadcast_to(inverse, inv_kept.shape[1:])

        def project(c, pre):
            x = xbuf[m, :, cols(c)].astype(jnp.float32)
            n = (x * inverse * gain[:, cols(c)]).astype(jnp.bfloat16)
            normed[m, :, cols(c)] = n
            return pre + jnp.dot(n, w_in[cols(c), :], preferred_element_type=jnp.float32)

        pre = lax.fori_loop(
            0, chunks, project, jnp.zeros((rows, w_in.shape[1]), jnp.float32), unroll=UNROLL
        )
        pre_kept[m] = pre
        hidden = jax.nn.silu(pre).astype(jnp.bfloat16)
        hidden_kept[m] = hidden

        @pl.when(stage < last)
        def _():
            def emit(c, carry):
                x = xbuf[m, :, cols(c)].astype(jnp.float32)
                y = jnp.dot(hidden, w_out[:, cols(c)], preferred_element_type=jnp.float32)
                xsend[m, :, cols(c)] = (x + y).astype(jnp.bfloat16)
                return carry

            lax.fori_loop(0, chunks, emit, 0, unroll=UNROLL)
            pass_on(xsend, xbuf, x_sent, x_recv, m, stage + 1).start()

        spread_columns(normed, normed_all, n_sems, m)
        spread_whole(hidden_kept, hidden_all, h_sems, m)

    def backward(m):
        landed(ubuf.at[m], u_recv.at[m])
        contract = (((1,), (1,)), ((), ()))

        def collect(c, total):
            return total + lax.dot_general(
                ubuf[m, :, cols(c)],
                w_out[:, cols(c)],
                contract,
                preferred_element_type=jnp.float32,
            )

        grad_hidden = lax.fori_loop(
            0, chunks, collect, jnp.zeros((rows, w_in.shape[1]), jnp.float32), unroll=UNROLL
        )
        pre = pre_kept[m]
        sig = jax.nn.sigmoid(pre)
        grad_pre = (grad_hidden * sig * (1.0 + pre * (1.0 - sig))).astype(jnp.bfloat16)
        grad_kept[m] = grad_pre

        @pl.when(stage > 0)
        def _():
            inverse = inv_kept[m][:, :1]

            def scale(c, total):
                t = lax.dot_general(
                    grad_pre, w_in[cols(c), :], contract, preferred_element_type=jnp.float32
                )
                t = t * gain[:, cols(c)]
                back[:, cols(c)] = t
                xhat = xbuf[m, :, cols(c)].astype(jnp.float32) * inverse
                return total + jnp.sum(t * xhat, axis=-1, keepdims=True)

            total = lax.fori_loop(
                0, chunks, scale, jnp.zeros((rows, 1), jnp.float32), unroll=UNROLL
            )
            mean = total / width

            def emit(c, carry):
                xhat = xbuf[m, :, cols(c)].astype(jnp.float32) * inverse
                u = ubuf[m, :, cols(c)].astype(jnp.float32)
                usend[m, :, cols(c)] = (
                    u + inverse * (back[:, cols(c)] - xhat * mean)
                ).astype(jnp.bfloat16)
                return carry

            lax.fori_loop(0, chunks, emit, 0, unroll=UNROLL)
            pass_on(usend, ubuf, u_sent, u_recv, m, stage - 1).start()

        spread_columns(ubuf, up_all, p_sems, m)
        spread_whole(grad_kept, grad_all, g_sems, m)

    delay = jnp.minimum(2 * (last - stage), micro)

    def step(k, carry):
        @pl.when(k < micro)
        def _():
            forward(k)

        @pl.when((k >= delay) & (k < delay + micro))
        def _():
            backward(k - delay)

        return carry

    lax.fori_loop(0, micro + min(2 * last, micro), step, 0)

    for m in range(micro):

        @pl.when(stage < last)
        def _(m=m):
            pass_on(xsend, xbuf, x_sent, x_recv, m, stage + 1).wait_send()

        @pl.when(stage > 0)
        def _(m=m):
            pass_on(usend, ubuf, u_sent, u_recv, m, stage - 1).wait_send()

    if peers > 1:
        landed(normed_all.at[pl.ds(0, peers - 1)], n_sems.at[0])
        landed(up_all.at[pl.ds(0, peers - 1)], p_sems.at[0])
        landed(hidden_all.at[pl.ds(0, peers - 1)], h_sems.at[0])
        landed(grad_all.at[pl.ds(0, peers - 1)], g_sems.at[0])
    landed(normed_all, n_sems.at[1])
    landed(up_all, p_sems.at[1])
    landed(hidden_all, h_sems.at[1])
    landed(grad_all, g_sems.at[1])


def per_device(sections, peers, inputs, cotangent, plan_order, norm_gain, weight_in, weight_out):
    micro, rows, width = inputs.shape
    inner = weight_in.shape[2]
    share = width // peers
    ordered = jnp.take(inputs, plan_order, axis=0, mode="clip")
    wide, narrow = (micro, rows, width), (micro, rows, inner)
    half, full = jnp.bfloat16, jnp.float32
    dma = pltpu.SemaphoreType.DMA
    anywhere = pl.BlockSpec(memory_space=pl.ANY)
    local = pl.BlockSpec(memory_space=pltpu.VMEM)
    normed_all, up_all, hidden_all, grad_all = pl.pallas_call(
        functools.partial(train_kernel, sections, peers),
        out_shape=(
            jax.ShapeDtypeStruct((peers, micro, rows, share), half),
            jax.ShapeDtypeStruct((peers, micro, rows, share), half),
            jax.ShapeDtypeStruct((peers, micro, rows, inner), half),
            jax.ShapeDtypeStruct((peers, micro, rows, inner), half),
        ),
        in_specs=[anywhere, anywhere, local, local, local],
        out_specs=[anywhere] * 4,
        scratch_shapes=[pltpu.VMEM(wide, half)] * 5
        + [
            pltpu.VMEM((rows, width), full),
            pltpu.VMEM(narrow, full),
            pltpu.VMEM(narrow, half),
            pltpu.VMEM(narrow, half),
            pltpu.VMEM((micro, rows, 128), full),
        ]
        + [dma((micro,))] * 4
        + [dma((2,))] * 4,
        compiler_params=pltpu.CompilerParams(
            collective_id=0, has_side_effects=True, vmem_limit_bytes=60 * 1024 * 1024
        ),
    )(ordered, cotangent, norm_gain, weight_in[0], weight_out[0])
    tokens = peers * micro * rows
    total_in = jnp.einsum(
        "td,tr->dr",
        normed_all.reshape(tokens, share),
        grad_all.reshape(tokens, inner),
        preferred_element_type=full,
    )
    total_out = jnp.einsum(
        "tr,td->rd",
        hidden_all.reshape(tokens, inner),
        up_all.reshape(tokens, share),
        preferred_element_type=full,
    )
    return (total_in.astype(half)[None], total_out.astype(half)[None])


def solution(mesh):
    in_specs = (
        P(None, "dp", None),
        P(None, "dp", None),
        P(),
        P("pipe", None),
        P("pipe", None, None),
        P("pipe", None, None),
    )
    out_specs = (P("pipe", "dp", None), P("pipe", None, "dp"))
    return jax.shard_map(
        functools.partial(per_device, mesh.shape["pipe"], mesh.shape["dp"]),
        mesh=mesh,
        in_specs=in_specs,
        out_specs=out_specs,
        check_vma=False,
    )
```

time: 633 us -> 276 us (0.44); the launches traced: 626 us -> 276 us
  Pallas kernels: 0 us -> 263 us
  waiting for transfers between devices: 252 us -> 0 us
  matrix products: 198 us -> 8.08 us
  other arithmetic: 88.7 us -> 0.81 us
  starting transfers between devices: 31.4 us -> 0 us
  local copies, waits for them, and re-layouts: 23.4 us -> 3.6 us
  loops' own time: 18.5 us -> 0 us
  between operations: 14.1 us -> 0.66 us
    pallas_call x0 -> x1, Pallas kernels: none -> 263 us  [per_device(): pl.pallas_call(functools.partial(train_kernel, sections, peers), out_shap...]
    dot_general x38 -> x2, matrix products: 198 us -> 8.08 us  [the longest x1 5.3 us: per_device(): jnp.einsum('td,tr->dr', normed_all.reshape(tokens, share), grad_all.resha...]
    reduce_scatter x2 -> x0, waiting for transfers between devices: 185 us -> none  [the longest x1 93.8 us: per_device(): lax.psum_scatter(term_in.astype(jnp.bfloat16), 'dp', scatter_dimension=0,...]
    ppermute x18 -> x0, waiting for transfers between devices: 67.4 us -> none  [passed_along(): return lax.ppermute(value, axis, pairs)]
    dynamic_update_slice x27 -> x0, other arithmetic: 61.9 us -> none  [put_slot(): lax.dynamic_update_index_in_dim(buffer, jnp.where(active_flag, new_value,...]
    ppermute x18 -> x0, starting transfers between devices: 31.3 us -> none  [passed_along(): return lax.ppermute(value, axis, pairs)]
    another operation x2 -> x0, loops' own time: 18.5 us -> none  [the longest x1 17.3 us: per_device(): lax.fori_loop(0, tick_count, forward_tick, (empty_rows, buffer(model_widt...]
    dynamic_slice x27 -> x0, local copies, waits for them, and re-layouts: 15.3 us -> none  [the longest x18 9.87 us: pick_slot(): return lax.dynamic_index_in_dim(buffer, slot_index, 0, keepdims=False)]
  transfers between devices with their start and end apart: 20 -> 0, of which waited for: 11 -> 0; matrix products, arithmetic and copies ran while one was open for 16% -> 0% of each run, Pallas kernels for 0% -> 0%
where the time goes in v1:
time: 276 us
  Pallas kernels  263 us (95%)
  matrix products  8.08 us (3%)
  local copies, waits for them, and re-layouts  3.6 us (1%)
    pallas_call x1, Pallas kernels, per_device(): pl.pallas_call(functools.partial(train_kernel, sections, peers), out_shap...  263 us

profile of v1, /device:TPU:31, one launch (start us, length us, event | category | flops | bytes accessed | tf_op | source)
XLA Modules:
  0.0 276.0 jit_solution(8267599174346987731)
XLA Ops:
  0.6 0.0 copy-start
  0.6 0.8 pad_clamp_fusion
  1.5 1.1 copy-done
  2.5 2.5 gather_fusion
  5.0 262.8 %shard_map.77 = (bf16[8,6,32,1024]{3,2,1,0:T(8,128)(2,1)}, bf16[8,6,32,1024]{3,2,1,0:T(8,128)(2,1)}, bf16[8,6,32,512]{3,2,1,0:T(8,128)(2,1)}, bf16[8,6,32,512]{3,2,1,0:T(8,128)(2,1)}) custom-call(bf16[6,32,8192]{2,1,0:T(8,128)(2,1)} %gather_fusion, bf16[6,32,8192]{2,1,0:T(8,128)(2,1)} %cot_hbm.1, f32[1,8192]{1,0:T(1,128)} %gain.1, ...), custom_call_target="tpu_custom_call" | custom-call | tf_op jit(solution)/shard_map/pallas_call | solution.py:267
  267.9 0.0 copy-start.1
  267.9 0.0 copy-start.2
  267.9 5.3 %fusion = bf16[1,1024,512]{2,1,0:T(8,128)(2,1)} fusion(bf16[8,6,32,1024]{3,2,1,0:T(8,128)(2,1)} %get-tuple-element.6, bf16[8,6,32,512]{3,2,1,0:T(8,128)(2,1)} %get-tuple-element.7), kind=kOutput, calls=%fused_computation.3 | convolution fusion | flops 1611137024 | bytes 5767168 | tf_op jit(solution)/shard_map/td,tr->dr/dot_general | solution.py:292
  273.2 0.0 copy-done.1
  273.2 0.0 copy-done.2
  273.2 2.8 %fusion.1 = bf16[1,512,1024]{2,1,0:T(8,128)(2,1)} fusion(bf16[8,6,32,512]{3,2,1,0:T(8,128)(2,1)S(1)} %copy-done.2, bf16[8,6,32,1024]{3,2,1,0:T(8,128)(2,1)S(1)} %copy-done.1), kind=kOutput, calls=%fused_computation.4 | convolution fusion | flops 1611137024 | bytes 5767168 | tf_op jit(solution)/shard_map/tr,td->rd/dot_general | solution.py:298
Async XLA Ops:
  0.6 1.9 copy-start
  267.9 5.3 %copy-start.1 = (bf16[8,6,32,1024]{3,2,1,0:T(8,128)(2,1)S(1)}, bf16[8,6,32,1024]{3,2,1,0:T(8,128)(2,1)}, u32[]{:S(2)}) copy-start(bf16[8,6,32,1024]{3,2,1,0:T(8,128)(2,1)} %get-tuple-element.9) | copy-start | bytes 9437188
  267.9 5.3 %copy-start.2 = (bf16[8,6,32,512]{3,2,1,0:T(8,128)(2,1)S(1)}, bf16[8,6,32,512]{3,2,1,0:T(8,128)(2,1)}, u32[]{:S(2)}) copy-start(bf16[8,6,32,512]{3,2,1,0:T(8,128)(2,1)} %get-tuple-element.8) | copy-start | bytes 4718596

commit v2 on v1

--- a/solution.py
+++ b/solution.py
@@ -10,7 +10,8 @@
 EPSILON = 1e-05
 MESH = pl.DeviceIdType.MESH
 CHUNK = 1024
-UNROLL = 2
+UNROLL = 8
+PIECES = 4
 
 
 def landed(ref, sem):
@@ -34,7 +35,6 @@
     xsend,
     usend,
     normed,
-    back,
     pre_kept,
     hidden_kept,
     grad_kept,
@@ -55,6 +55,9 @@
     share = width // peers
     chunk = min(CHUNK, width)
     chunks = width // chunk
+    piece = width // PIECES
+    pieces = [pl.ds(p * piece, piece) for p in range(PIECES)]
+    per_piece = chunks // PIECES
 
     barrier = pltpu.get_barrier_semaphore()
     for j in range(1, peers):
@@ -77,15 +80,21 @@
     @pl.when(stage == 0)
     def _():
         for m in range(micro):
-            pltpu.make_async_copy(rows_hbm.at[m], xbuf.at[m], x_recv.at[m]).start()
+            for p, part in enumerate(pieces):
+                pltpu.make_async_copy(
+                    rows_hbm.at[m, :, part], xbuf.at[m, :, part], x_recv.at[m, p]
+                ).start()
 
     @pl.when(stage == last)
     def _():
         for m in range(micro):
-            pltpu.make_async_copy(cot_hbm.at[m], ubuf.at[m], u_recv.at[m]).start()
+            for p, part in enumerate(pieces):
+                pltpu.make_async_copy(
+                    cot_hbm.at[m, :, part], ubuf.at[m, :, part], u_recv.at[m, p]
+                ).start()
 
     def cols(c):
-        return pl.ds(pl.multiple_of(c * chunk, chunk), chunk)
+        return pl.ds(c * chunk, chunk) if isinstance(c, int) else pl.ds(pl.multiple_of(c * chunk, chunk), chunk)
 
     def spread_columns(source, target, sems, m):
         for j in range(1, peers):
@@ -116,25 +125,36 @@
             ).start()
         pltpu.make_async_copy(source.at[m], target.at[me, m], sems.at[1]).start()
 
-    def pass_on(source, target, send, recv, m, to):
+    def pass_on(source, target, send, recv, m, p, to):
         return pltpu.make_async_remote_copy(
-            src_ref=source.at[m],
-            dst_ref=target.at[m],
-            send_sem=send.at[m],
-            recv_sem=recv.at[m],
+            src_ref=source.at[m, :, pieces[p]],
+            dst_ref=target.at[m, :, pieces[p]],
+            send_sem=send.at[m, p],
+            recv_sem=recv.at[m, p],
             device_id={"pipe": to},
             device_id_type=MESH,
         )
 
+    def by_piece(run, first, before=None, after=None):
+        value = first
+        for p in range(PIECES):
+            if before is not None:
+                before(p)
+            for c in range(p * per_piece, (p + 1) * per_piece):
+                value = run(c, value)
+            if after is not None:
+                after(p)
+        return value
+
     def forward(m):
-        landed(xbuf.at[m], x_recv.at[m])
-
         def square(c, total):
             x = xbuf[m, :, cols(c)].astype(jnp.float32)
             return total + jnp.sum(x * x, axis=-1, keepdims=True)
 
-        total = lax.fori_loop(
-            0, chunks, square, jnp.zeros((rows, 1), jnp.float32), unroll=UNROLL
+        total = by_piece(
+            square,
+            jnp.zeros((rows, 1), jnp.float32),
+            before=lambda p: landed(xbuf.at[m, :, pieces[p]], x_recv.at[m, p]),
         )
         inverse = lax.rsqrt(total / width + EPSILON)
         inv_kept[m] = jnp.broadcast_to(inverse, inv_kept.shape[1:])
@@ -160,14 +180,18 @@
                 xsend[m, :, cols(c)] = (x + y).astype(jnp.bfloat16)
                 return carry
 
-            lax.fori_loop(0, chunks, emit, 0, unroll=UNROLL)
-            pass_on(xsend, xbuf, x_sent, x_recv, m, stage + 1).start()
+            by_piece(
+                emit,
+                0,
+                after=lambda p: pass_on(
+                    xsend, xbuf, x_sent, x_recv, m, p, stage + 1
+                ).start(),
+            )
 
         spread_columns(normed, normed_all, n_sems, m)
         spread_whole(hidden_kept, hidden_all, h_sems, m)
 
     def backward(m):
-        landed(ubuf.at[m], u_recv.at[m])
         contract = (((1,), (1,)), ((), ()))
 
         def collect(c, total):
@@ -178,9 +202,12 @@
                 preferred_element_type=jnp.float32,
             )
 
-        grad_hidden = lax.fori_loop(
-            0, chunks, collect, jnp.zeros((rows, w_in.shape[1]), jnp.float32), unroll=UNROLL
-        )
+        grad_hidden = by_piece(
+            collect,
+            jnp.zeros((rows, w_in.shape[1]), jnp.float32),
+            before=lambda p: landed(ubuf.at[m, :, pieces[p]], u_recv.at[m, p]),
+        )
+        spread_columns(ubuf, up_all, p_sems, m)
         pre = pre_kept[m]
         sig = jax.nn.sigmoid(pre)
         grad_pre = (grad_hidden * sig * (1.0 + pre * (1.0 - sig))).astype(jnp.bfloat16)
@@ -190,32 +217,26 @@
         def _():
             inverse = inv_kept[m][:, :1]
 
-            def scale(c, total):
+            mean = jnp.sum(grad_pre.astype(jnp.float32) * pre, axis=-1, keepdims=True) / width
+
+            def emit(c, carry):
                 t = lax.dot_general(
                     grad_pre, w_in[cols(c), :], contract, preferred_element_type=jnp.float32
                 )
                 t = t * gain[:, cols(c)]
-                back[:, cols(c)] = t
-                xhat = xbuf[m, :, cols(c)].astype(jnp.float32) * inverse
-                return total + jnp.sum(t * xhat, axis=-1, keepdims=True)
-
-            total = lax.fori_loop(
-                0, chunks, scale, jnp.zeros((rows, 1), jnp.float32), unroll=UNROLL
-            )
-            mean = total / width
-
-            def emit(c, carry):
                 xhat = xbuf[m, :, cols(c)].astype(jnp.float32) * inverse
                 u = ubuf[m, :, cols(c)].astype(jnp.float32)
-                usend[m, :, cols(c)] = (
-                    u + inverse * (back[:, cols(c)] - xhat * mean)
-                ).astype(jnp.bfloat16)
+                usend[m, :, cols(c)] = (u + inverse * (t - xhat * mean)).astype(jnp.bfloat16)
                 return carry
 
-            lax.fori_loop(0, chunks, emit, 0, unroll=UNROLL)
-            pass_on(usend, ubuf, u_sent, u_recv, m, stage - 1).start()
-
-        spread_columns(ubuf, up_all, p_sems, m)
+            by_piece(
+                emit,
+                0,
+                after=lambda p: pass_on(
+                    usend, ubuf, u_sent, u_recv, m, p, stage - 1
+                ).start(),
+            )
+
         spread_whole(grad_kept, grad_all, g_sems, m)
 
     delay = jnp.minimum(2 * (last - stage), micro)
@@ -237,11 +258,13 @@
 
         @pl.when(stage < last)
         def _(m=m):
-            pass_on(xsend, xbuf, x_sent, x_recv, m, stage + 1).wait_send()
+            for p in range(PIECES):
+                pass_on(xsend, xbuf, x_sent, x_recv, m, p, stage + 1).wait_send()
 
         @pl.when(stage > 0)
         def _(m=m):
-            pass_on(usend, ubuf, u_sent, u_recv, m, stage - 1).wait_send()
+            for p in range(PIECES):
+                pass_on(usend, ubuf, u_sent, u_recv, m, p, stage - 1).wait_send()
 
     if peers > 1:
         landed(normed_all.at[pl.ds(0, peers - 1)], n_sems.at[0])
@@ -276,13 +299,12 @@
         out_specs=[anywhere] * 4,
         scratch_shapes=[pltpu.VMEM(wide, half)] * 5
         + [
-            pltpu.VMEM((rows, width), full),
             pltpu.VMEM(narrow, full),
             pltpu.VMEM(narrow, half),
             pltpu.VMEM(narrow, half),
             pltpu.VMEM((micro, rows, 128), full),
         ]
-        + [dma((micro,))] * 4
+        + [dma((micro, PIECES))] * 4
         + [dma((2,))] * 4,
         compiler_params=pltpu.CompilerParams(
             collective_id=0, has_side_effects=True, vmem_limit_bytes=60 * 1024 * 1024

time: 276 us -> 270 us (0.978)
  Pallas kernels: 263 us -> 257 us
    pallas_call x1, Pallas kernels: 263 us -> 257 us  [per_device(): pl.pallas_call(functools.partial(train_kernel, sections, peers), out_shap...]
where the time goes in v2:
time: 270 us
  Pallas kernels  257 us (95%)
  matrix products  8.08 us (3%)
  local copies, waits for them, and re-layouts  3.6 us (1%)
    pallas_call x1, Pallas kernels, per_device(): pl.pallas_call(functools.partial(train_kernel, sections, peers), out_shap...  257 us

profile of v2, /device:TPU:31, one launch (start us, length us, event | category | flops | bytes accessed | tf_op | source)
XLA Modules:
  0.0 269.9 jit_solution(4445997835640515341)
XLA Ops:
  0.6 0.0 copy-start
  0.6 0.8 pad_clamp_fusion
  1.5 1.1 copy-done
  2.5 2.5 gather_fusion
  5.0 256.7 %shard_map.77 = (bf16[8,6,32,1024]{3,2,1,0:T(8,128)(2,1)}, bf16[8,6,32,1024]{3,2,1,0:T(8,128)(2,1)}, bf16[8,6,32,512]{3,2,1,0:T(8,128)(2,1)}, bf16[8,6,32,512]{3,2,1,0:T(8,128)(2,1)}) custom-call(bf16[6,32,8192]{2,1,0:T(8,128)(2,1)} %gather_fusion, bf16[6,32,8192]{2,1,0:T(8,128)(2,1)} %cot_hbm.1, f32[1,8192]{1,0:T(1,128)} %gain.1, ...), custom_call_target="tpu_custom_call" | custom-call | tf_op jit(solution)/shard_map/pallas_call | solution.py:290
  261.8 0.0 copy-start.1
  261.8 0.0 copy-start.2
  261.8 5.3 %fusion = bf16[1,1024,512]{2,1,0:T(8,128)(2,1)} fusion(bf16[8,6,32,1024]{3,2,1,0:T(8,128)(2,1)} %get-tuple-element.6, bf16[8,6,32,512]{3,2,1,0:T(8,128)(2,1)} %get-tuple-element.7), kind=kOutput, calls=%fused_computation.3 | convolution fusion | flops 1611137024 | bytes 5767168 | tf_op jit(solution)/shard_map/td,tr->dr/dot_general | solution.py:314
  267.1 0.0 copy-done.1
  267.1 0.0 copy-done.2
  267.1 2.8 %fusion.1 = bf16[1,512,1024]{2,1,0:T(8,128)(2,1)} fusion(bf16[8,6,32,512]{3,2,1,0:T(8,128)(2,1)S(1)} %copy-done.2, bf16[8,6,32,1024]{3,2,1,0:T(8,128)(2,1)S(1)} %copy-done.1), kind=kOutput, calls=%fused_computation.4 | convolution fusion | flops 1611137024 | bytes 5767168 | tf_op jit(solution)/shard_map/tr,td->rd/dot_general | solution.py:320
Async XLA Ops:
  0.6 1.9 copy-start
  261.8 5.3 %copy-start.1 = (bf16[8,6,32,1024]{3,2,1,0:T(8,128)(2,1)S(1)}, bf16[8,6,32,1024]{3,2,1,0:T(8,128)(2,1)}, u32[]{:S(2)}) copy-start(bf16[8,6,32,1024]{3,2,1,0:T(8,128)(2,1)} %get-tuple-element.9) | copy-start | bytes 9437188
  261.8 5.3 %copy-start.2 = (bf16[8,6,32,512]{3,2,1,0:T(8,128)(2,1)S(1)}, bf16[8,6,32,512]{3,2,1,0:T(8,128)(2,1)}, u32[]{:S(2)}) copy-start(bf16[8,6,32,512]{3,2,1,0:T(8,128)(2,1)} %get-tuple-element.8) | copy-start | bytes 4718596
